TPU v7x, 128 devices: a whole 4x4x4 slice. The times are simulated.
128 devices in a mesh: rec: 4 (over z), tm: 32 (over x, y, core).
Axes of the slice: x: 4, y: 4, z: 4, core: 2. Of those that a mesh axis runs over, the one named last changes fastest.
Arguments:
- mel_frames: bfloat16 [4, 65536, 80], P('rec', 'tm'), may hold values from -6 to 6
- lengths: int32 [4, 4], P('rec'), may hold values from 1 to 32768, 65536 in all within a row
- w_first: float32 [3, 3, 256], replicated, may hold values from -2 to 2
- w_second: bfloat16 [2304, 256], P(('rec', 'tm')), may hold values from -0.125 to 0.125
- w_proj: bfloat16 [5120, 1024], P(('rec', 'tm')), may hold values from -0.078125 to 0.078125
- gain_attn: float32 [1024], replicated, may hold values from 0.5 to 1.5
- w_qkv: bfloat16 [1024, 3072], P(('rec', 'tm')), may hold values from -2 to 2
- w_out: bfloat16 [1024, 1024], P(('rec', 'tm')), may hold values from -0.1875 to 0.1875
- gain_conv: float32 [1024], replicated, may hold values from 0.5 to 1.5
- w_point_in: bfloat16 [1024, 2048], P(('rec', 'tm')), may hold values from -0.1875 to 0.1875
- w_depth: float32 [9, 1024], replicated, may hold values from -6 to 6
- w_point_out: bfloat16 [1024, 1024], P(('rec', 'tm')), may hold values from -0.375 to 0.375
- gain_out: float32 [1024], replicated, may hold values from 0.5 to 1.5
Outputs:
- encoded: bfloat16 [4, 16384, 1024], P('rec', 'tm')
Inputs may be any that keep to these rules, and one draw needn't show every extreme that they name: Each group's 4 lengths sum to 65536, and the largest of them is 32768.
All inputs are finite; a program needn't handle non-finite values.
Results may differ from a plain program's by a relative error of at most 0.024.
The roundings to bfloat16 on the way count: a program that leaves them out, or rounds other values in their place, can miss the bound.
Values may be sent and summed in bfloat16 or wider, within the bound.
A program may use at most 128 MiB of HBM per device.

v0:
```python
import jax
import jax.numpy as jnp
from jax import lax
from jax.sharding import PartitionSpec as P

WIDTH = 1024
HEADS = 8
KERNEL = 9
WINDOW = 128
CONV_BLOCK = 64
HEAD_DIM = 128
NORM_EPSILON = 1e-05


def passed_along(block, axis, distance):
    devices = range(lax.axis_size(axis))
    route = [(i - distance, i) for i in devices if i - distance in devices]
    return lax.ppermute(block, axis, route)


def with_halo(block, sides, width):
    for axis, dim in sides:
        count = lax.axis_size(axis)
        forward = [(i, i + 1) for i in range(count - 1)]
        backward = [(target, source) for source, target in forward]
        low = lax.ppermute(
            lax.slice_in_dim(block, block.shape[dim] - width, None, axis=dim), axis, forward
        )
        high = lax.ppermute(lax.slice_in_dim(block, 0, width, axis=dim), axis, backward)
        block = jnp.concatenate([low, block, high], axis=dim)
    return block


def layer_norm(values, gain):
    row_mean = jnp.mean(values, axis=-1, keepdims=True)
    centred = values - row_mean
    variance = jnp.mean(centred * centred, axis=-1, keepdims=True)
    return centred * lax.rsqrt(variance + NORM_EPSILON) * gain


def segment_ids(positions, bounds, limit):
    counted = jnp.sum((positions[:, None] >= bounds[None, :-1]).astype(jnp.int32), axis=1)
    inside = (positions >= 0) & (positions < limit)
    return jnp.where(inside, counted, -1)


def conv_first(window, seg_rows, w_first):
    frame_count = (window.shape[0] - 1) // 2
    bins = window.shape[1]
    padded = jnp.pad(window.astype(jnp.float32), ((0, 0), (1, 1)))
    centre = seg_rows[1 : 2 * frame_count : 2]
    total = jnp.zeros((frame_count, bins // 2, w_first.shape[-1]), jnp.float32)
    for step_t in range(3):
        taken = padded[step_t : step_t + 2 * frame_count - 1 : 2]
        same_seg = (seg_rows[step_t : step_t + 2 * frame_count - 1 : 2] == centre).astype(
            jnp.float32
        )
        taken = taken * same_seg[:, None]
        for step_f in range(3):
            columns = taken[:, step_f : step_f + bins - 1 : 2]
            total = total + columns[:, :, None] * w_first[step_t, step_f][None, None, :]
    return jnp.maximum(total, 0.0).astype(jnp.bfloat16)


def conv_second(first, seg_first, w_second):
    frame_count = (first.shape[0] - 1) // 2
    channels = first.shape[2]
    quarter = first.shape[1] // 2
    padded = jnp.pad(first, ((0, 0), (1, 1), (0, 0)))
    centre = seg_first[1 : 2 * frame_count : 2]
    total = jnp.zeros((frame_count * quarter, w_second.shape[1]), jnp.float32)
    for step_t in range(3):
        taken = padded[step_t : step_t + 2 * frame_count - 1 : 2]
        same_seg = (seg_first[step_t : step_t + 2 * frame_count - 1 : 2] == centre).astype(
            jnp.bfloat16
        )
        taken = taken * same_seg[:, None, None]
        for step_f in range(3):
            columns = taken[:, step_f : step_f + 2 * quarter - 1 : 2].reshape(
                frame_count * quarter, channels
            )
            offset = (step_t * 3 + step_f) * channels
            total = total + jnp.dot(
                columns, w_second[offset : offset + channels], preferred_element_type=jnp.float32
            )
    return jnp.maximum(total, 0.0).astype(jnp.bfloat16).reshape(frame_count, quarter * channels)


def attend_block(q_block, kv_block, q_seg, k_seg):
    row_count = q_block.shape[0]
    span = kv_block.shape[0]
    reach = (span - row_count) // 2
    offsets = (
        jnp.arange(span, dtype=jnp.int32)[None, :]
        - jnp.arange(row_count, dtype=jnp.int32)[:, None]
        - reach
    )
    allowed = (jnp.abs(offsets) <= reach) & (k_seg[None, :] == q_seg[:, None])

    def one_head(head):
        start = head * HEAD_DIM
        q_head = lax.dynamic_slice_in_dim(q_block, start, HEAD_DIM, 1)
        k_head = lax.dynamic_slice_in_dim(kv_block, start, HEAD_DIM, 1)
        v_head = lax.dynamic_slice_in_dim(kv_block, WIDTH + start, HEAD_DIM, 1)
        scores = lax.dot_general(
            q_head, k_head, (((1,), (1,)), ((), ())), preferred_element_type=jnp.float32
        ) * HEAD_DIM ** (-0.5)
        scores = jnp.where(allowed, scores, -1e30)
        row_max = jnp.max(scores, axis=-1, keepdims=True)
        exped = jnp.where(allowed, jnp.exp(scores - row_max), 0.0)
        probabilities = (exped / jnp.sum(exped, axis=-1, keepdims=True)).astype(jnp.bfloat16)
        return jnp.dot(probabilities, v_head, preferred_element_type=jnp.float32).astype(
            jnp.bfloat16
        )

    per_head = lax.map(one_head, jnp.arange(HEADS, dtype=jnp.int32))
    return jnp.transpose(per_head, (1, 0, 2)).reshape(row_count, WIDTH)


def depthwise(gated_ext, seg_ext, seg_mid, w_depth):
    length = seg_mid.shape[0]
    total = jnp.zeros((length, gated_ext.shape[1]), jnp.float32)
    for tap_index in range(w_depth.shape[0]):
        same_seg = (seg_ext[tap_index : tap_index + length] == seg_mid).astype(jnp.float32)
        total = (
            total
            + gated_ext[tap_index : tap_index + length].astype(jnp.float32)
            * w_depth[tap_index][None, :]
            * same_seg[:, None]
        )
    return jax.nn.silu(total).astype(jnp.bfloat16)


def add_product(inputs, piece):
    return jnp.dot(inputs, piece, preferred_element_type=jnp.float32)


def on_device(
    mel_frames,
    lengths,
    w_first,
    w_second,
    w_proj,
    gain_attn,
    w_qkv,
    w_out,
    gain_conv,
    w_point_in,
    w_depth,
    w_point_out,
    gain_out,
):
    frames_dev = mel_frames.shape[1]
    tokens_dev = frames_dev // 4
    shards = lax.axis_size("tm")
    index = lax.axis_index("tm")
    frames_all = frames_dev * shards
    bounds = jnp.cumsum(lengths[0])
    local_mel = mel_frames[0]
    first_base = index * frames_dev
    second_full = lax.all_gather(w_second, ("rec", "tm"), axis=0, tiled=True)
    block_count = tokens_dev // CONV_BLOCK
    mel_edge = passed_along(local_mel[frames_dev - 3 :], "tm", 1)
    extended = jnp.concatenate([mel_edge, local_mel], axis=0)

    def sub_block(block):
        start = block * CONV_BLOCK
        window = lax.dynamic_slice_in_dim(extended, 4 * start, 4 * CONV_BLOCK + 3, 0)
        positions = first_base + 4 * start - 3 + jnp.arange(4 * CONV_BLOCK + 3, dtype=jnp.int32)
        seg_rows = segment_ids(positions, bounds, frames_all)
        first = conv_first(window, seg_rows, w_first)
        return conv_second(first, seg_rows[1::2], second_full)

    sub = lax.map(sub_block, jnp.arange(block_count, dtype=jnp.int32))
    sub = sub.reshape(tokens_dev, sub.shape[-1])
    hidden = add_product(sub, lax.all_gather(w_proj, ("rec", "tm"), axis=0, tiled=True))
    token_pos = index * tokens_dev + jnp.arange(tokens_dev, dtype=jnp.int32)
    token_seg = segment_ids(4 * token_pos, bounds, frames_all)
    key_pos = index * tokens_dev - WINDOW + jnp.arange(tokens_dev + 2 * WINDOW, dtype=jnp.int32)
    key_seg = segment_ids(4 * key_pos, bounds, frames_all)
    normed = layer_norm(hidden, gain_attn).astype(jnp.bfloat16)
    mixed = add_product(normed, lax.all_gather(w_qkv, ("rec", "tm"), axis=0, tiled=True)).astype(
        jnp.bfloat16
    )
    query = mixed[:, :WIDTH]
    keyval = with_halo(mixed[:, WIDTH:], (("tm", 0),), WINDOW)
    block_rows = min(512, tokens_dev)
    block = 0
    start = block * block_rows
    pieces = attend_block(query, keyval, token_seg, key_seg)
    attn_out = add_product(pieces, lax.all_gather(w_out, ("rec", "tm"), axis=0, tiled=True))
    attended = hidden + attn_out
    normed_conv = layer_norm(attended, gain_conv).astype(jnp.bfloat16)
    upward = add_product(normed_conv, lax.all_gather(w_point_in, ("rec", "tm"), axis=0, tiled=True))
    gated = (upward[:, :WIDTH] * jax.nn.sigmoid(upward[:, WIDTH:])).astype(jnp.bfloat16)
    reach = KERNEL // 2
    gated_ext = with_halo(gated, (("tm", 0),), KERNEL // 2)
    depth_pos = index * tokens_dev - reach + jnp.arange(tokens_dev + 2 * reach, dtype=jnp.int32)
    seg_ext = segment_ids(4 * depth_pos, bounds, frames_all)
    acted = depthwise(gated_ext, seg_ext, token_seg, w_depth)
    conv_out = add_product(acted, lax.all_gather(w_point_out, ("rec", "tm"), axis=0, tiled=True))
    combined = attended + conv_out
    return layer_norm(combined, gain_out).astype(jnp.bfloat16)[None]


def solution(mesh):
    placed = (
        P("rec", "tm", None),
        P("rec", None),
        P(),
        P(("rec", "tm"), None),
        P(("rec", "tm"), None),
        P(),
        P(("rec", "tm"), None),
        P(("rec", "tm"), None),
        P(),
        P(("rec", "tm"), None),
        P(),
        P(("rec", "tm"), None),
        P(),
    )
    return jax.shard_map(
        on_device, mesh=mesh, in_specs=placed, out_specs=P("rec", "tm", None), check_vma=False
    )
```

profile of v0, /device:TPU:25, one launch (start us, length us, event | category | flops | bytes accessed | tf_op | source)
XLA Modules:
  0.0 880.1 jit_solution(9001724628954924536)
XLA Ops:
  18.9 56.1 %all-gather.18.cloned.1.call-done = bf16[128,18,256]{2,1,0:T(8,128)(2,1)} async-done(((bf16[1,18,256]{2,1,0:T(8,128)(2,1)}), bf16[128,18,256]{2,1,0:T(8,128)(2,1)}) %all-gather.18.cloned.1.call-update) | async-done | bytes 1179664 | tf_op jit(solution)/shard_map/all_gather | solution.py:161
  78.8 684.2 %while.25 = (s32[]{:T(128)}, bf16[8,64,5120]{2,1,0:T(8,128)(2,1)}, s32[8]{0:T(128)}, bf16[2051,80]{1,0:T(8,128)(2,1)}, s32[]{:T(128)}, /*index=5*/s32[4]{0:T(128...) while((s32[]{:T(128)}, bf16[8,64,5120]{2,1,0:T(8,128)(2,1)}, ...), condition=%wide.region_3.4_spmd, body=%wide.region_1.3_spmd.sunk | while | flops 1543876352 | bytes 92566552 | solution.py:174
  90.5 7.7 maximum_convert_fusion.2
  101.9 6.9 slice.735
  114.6 4.9 slice.737
  123.2 4.8 slice.738
  135.1 4.9 slice.740
  143.8 4.8 slice.741
  155.5 4.9 slice.743
  176.2 7.7 maximum_convert_fusion.2
  187.6 6.9 slice.735
  200.4 4.9 slice.737
  209.1 4.8 slice.738
  220.8 4.9 slice.740
  229.4 4.8 slice.741
  241.1 4.9 slice.743
  261.8 7.7 maximum_convert_fusion.2
  273.2 6.9 slice.735
  286.0 4.9 slice.737
  294.6 4.8 slice.738
  306.3 4.9 slice.740
  314.9 4.8 slice.741
  326.6 4.9 slice.743
  347.3 7.7 maximum_convert_fusion.2
  358.7 6.9 slice.735
  371.5 4.9 slice.737
  380.0 4.8 slice.738
  391.8 4.9 slice.740
  400.4 4.8 slice.741
  412.1 4.9 slice.743
  432.8 7.7 maximum_convert_fusion.2
  444.2 6.9 slice.735
  457.0 4.9 slice.737
  465.5 4.8 slice.738
  477.3 4.9 slice.740
  485.9 4.8 slice.741
  497.6 4.9 slice.743
  518.3 7.7 maximum_convert_fusion.2
  529.7 6.9 slice.735
  542.4 4.9 slice.737
  551.0 4.8 slice.738
  562.7 4.9 slice.740
  571.4 4.8 slice.741
  583.0 4.9 slice.743
  603.7 7.7 maximum_convert_fusion.2
  615.1 6.9 slice.735
  627.9 4.9 slice.737
  636.5 4.8 slice.738
  648.2 4.9 slice.740
  656.8 4.8 slice.741
  668.5 4.9 slice.743
  689.2 7.7 maximum_convert_fusion.2
  700.6 6.9 slice.735
  713.3 4.9 slice.737
  721.9 4.8 slice.738
  733.6 4.9 slice.740
  742.3 4.8 slice.741
  754.0 4.9 slice.743
  763.0 10.0 %fusion.62 = (f32[512]{0:T(512)S(1)}, f32[512,1024]{1,0:T(8,128)S(1)}) fusion(bf16[512,5120]{1,0:T(8,128)(2,1)} %bitcast.117, bf16[5120,1024]{1,0:T(8,128)(2,1)} %all-gather.8.cloned.1.call-done), kind=kOutput, calls=%fused_computation.140 | convolution fusion | flops 5369232896 | bytes 17827840 | tf_op jit(solution)/shard_map/dot_general | solution.py:135
  773.7 6.6 convolution_convert_fusion.1
  790.5 6.5 collective-permute-done.2
  798.8 47.7 %while.26 = (s32[]{:T(128)}, bf16[8,512,128]{1,2,0:T(8,128)(2,1)}, s32[8]{0:T(128)S(1)}, bf16[512,1024]{1,0:T(8,128)(2,1)S(1)}, bf16[768,2048]{1,0:T(8,128)(2,1)...) while((s32[]{:T(128)}, bf16[8,512,128]{1,2,0:T(8,128)(2,1)}, ...), condition=%wide.region_11.12_spmd.clone, body=%wide.region_8.11_spmd.clone.sunk | while | flops 212401152 | bytes 5925630 | solution.py:116
  851.1 4.6 fusion.38
  865.3 6.0 fusion.64
  (639 shorter events, 453.6 us)
Async XLA Ops:
  6.5 68.5 %all-gather.18.cloned.1.call-start = ((), (), s32[]{:S(2)}) async-start(), calls=%async_computation.5 | async-start | bytes 1585152 | tf_op jit(solution)/shard_map/all_gather | solution.py:161
  7.3 755.7 %all-gather.8.cloned.1.call-start = ((), (), s32[]{:S(2)}) async-start(), calls=%async_computation | async-start | bytes 10567680 | tf_op jit(solution)/shard_map/all_gather | solution.py:176
  8.0 765.4 %all-gather.10.cloned.1.call-start = ((), (), s32[]{:S(2)}) async-start(), calls=%async_computation.1 | async-start | bytes 6340608 | tf_op jit(solution)/shard_map/all_gather | solution.py:182
  8.7 837.7 %all-gather.12.cloned.1.call-start = ((), (), s32[]{:S(2)}) async-start(), calls=%async_computation.2 | async-start | bytes 2113536 | tf_op jit(solution)/shard_map/all_gather | solution.py:191
  9.3 841.5 %all-gather.14.cloned.1.call-start = ((), (), s32[]{:S(2)}) async-start(), calls=%async_computation.3 | async-start | bytes 4227072 | tf_op jit(solution)/shard_map/all_gather | solution.py:194
  9.9 851.0 %all-gather.16.cloned.1.call-start = ((), (), s32[]{:S(2)}) async-start(), calls=%async_computation.4 | async-start | bytes 2113536 | tf_op jit(solution)/shard_map/all_gather | solution.py:201
  11.2 67.6 %copy-start.7 = (f32[3,3,256]{2,1,0:T(4,128)S(1)}, f32[3,3,256]{2,1,0:T(4,128)}, u32[]{:S(2)}) copy-start(f32[3,3,256]{2,1,0:T(4,128)} %param.19) | copy-start | bytes 27652
  11.2 6.7 collective-permute-start
  16.6 62.2 %copy-start.11 = (s32[3]{0:T(128)}, s32[3]{0:T(128)S(1)}, u32[]{:S(2)}) copy-start(s32[3]{0:T(128)S(1)} %slice_bitcast_fusion.1) | copy-start | bytes 40
  108.8 2.5 copy-start.2
  119.5 3.7 copy-start.1
  123.2 6.2 copy-start.4
  140.1 3.8 copy-start
  143.8 6.0 copy-start.3
  194.5 2.5 copy-start.2
  205.3 3.8 copy-start.1
  209.1 6.0 copy-start.4
  225.7 3.7 copy-start
  229.4 6.0 copy-start.3
  280.1 2.5 copy-start.2
  290.9 3.7 copy-start.1
  294.6 6.0 copy-start.4
  311.2 3.7 copy-start
  314.9 6.0 copy-start.3
  365.6 2.5 copy-start.2
  376.4 3.7 copy-start.1
  380.0 6.0 copy-start.4
  396.7 3.7 copy-start
  400.4 6.0 copy-start.3
  451.1 2.5 copy-start.2
  461.9 3.7 copy-start.1
  465.5 6.0 copy-start.4
  482.2 3.7 copy-start
  485.9 6.0 copy-start.3
  536.5 2.5 copy-start.2
  547.3 3.7 copy-start.1
  551.0 6.0 copy-start.4
  567.6 3.7 copy-start
  571.3 6.0 copy-start.3
  622.0 2.5 copy-start.2
  632.8 3.7 copy-start.1
  636.4 6.0 copy-start.4
  653.1 3.7 copy-start
  656.8 6.0 copy-start.3
  707.4 2.5 copy-start.2
  718.2 3.7 copy-start.1
  721.9 6.0 copy-start.4
  738.6 3.7 copy-start
  742.3 6.0 copy-start.3
  773.0 7.3 copy-start.6
  773.0 0.7 copy-start.14
  780.3 6.4 copy-start.5
  780.3 6.0 copy-start.10
  780.3 6.0 copy-start.12
  780.3 6.1 copy-start.8
  780.3 6.1 copy-start.9
  780.4 10.1 %collective-permute-start.1 = (bf16[128,2048]{1,0:T(8,128)(2,1)S(1)}, bf16[128,2048]{1,0:T(8,128)(2,1)S(1)}, u32[]{:S(2)}, u32[]{:S(2)}) collective-permute-start(bf16[128,2048]{1,0:T(8,128)(2,1)S(1)} %get-tuple-element.258), channel_id=1, source_target_pairs={{0,1},{1,2},{2,3},{3,4},{4,5},{5,6},{6,7},{7,8},{8,9},{9,10},{10,1... | collective-permute-start | bytes 1572872 | tf_op jit(solution)/shard_map/ppermute | solution.py:26
  784.4 12.6 %collective-permute-start.2 = (bf16[128,2048]{1,0:T(8,128)(2,1)S(1)}, bf16[128,2048]{1,0:T(8,128)(2,1)S(1)}, u32[]{:S(2)}, u32[]{:S(2)}) collective-permute-start(bf16[128,2048]{1,0:T(8,128)(2,1)S(1)} %get-tuple-element.259), channel_id=1, source_target_pairs={{1,0},{2,1},{3,2},{4,3},{5,4},{6,5},{7,6},{8,7},{9,8},{10,9},{11,1... | collective-permute-start | bytes 1572872 | tf_op jit(solution)/shard_map/ppermute | solution.py:29
  786.7 12.1 %slice-start = ((bf16[512,3072]{1,0:T(8,128)(2,1)}), bf16[512,1024]{1,0:T(8,128)(2,1)S(1)}, s32[]{:S(2)}) async-start(bf16[512,3072]{1,0:T(8,128)(2,1)} %copy-done.5), calls=%async_computation.6 | async-start | bytes 2097152 | tf_op jit(solution)/shard_map/slice | solution.py:185
  850.4 0.7 copy-start.15
  856.3 4.7 collective-permute-start.3
  858.2 7.1 collective-permute-start.4
  871.3 0.7 copy-start.13
Sparse Core Ops, SparseCore 0:
  10.2 64.8 all-gather.17
  78.2 70.0 all-gather.7
  151.5 65.5 all-gather.9
  220.0 62.7 all-gather.11
  285.8 64.3 all-gather.13
  353.1 62.7 all-gather.15
where the time goes:
time: 886 us; the launch traced here: 880 us
  local copies, waits for them, and re-layouts  458 us (52%)
  matrix products  202 us (23%)
  other arithmetic  106 us (12%)
  waiting for transfers between devices  74 us (8%)
  starting transfers between devices  14 us (2%)
  between operations  13.8 us (2%)
  loops' own time  12.6 us (1%)
    slice x72, local copies, waits for them, and re-layouts, conv_second(): taken[:, step_f:step_f + 2 * quarter - 1:2]  284 us
    dot_general x72, matrix products, conv_second(): jnp.dot(columns, w_second[offset:offset + channels], preferred_element_ty...  145 us
    convert_element_type x8, other arithmetic, conv_first(): return jnp.maximum(total, 0.0).astype(jnp.bfloat16)  61.5 us
    slice x72, local copies, waits for them, and re-layouts, conv_first(): columns = taken[:, step_f:step_f + bins - 1:2]  57.2 us
    reshape x72, local copies, waits for them, and re-layouts, conv_second(): taken[:, step_f:step_f + 2 * quarter - 1:2]  56.1 us
    all_gather x1, waiting for transfers between devices, on_device(): second_full = lax.all_gather(w_second, ('rec', 'tm'), axis=0, tiled=True)  56.1 us
    dot_general x5, matrix products, add_product(): return jnp.dot(inputs, piece, preferred_element_type=jnp.float32)  31 us
    mul x8, other arithmetic, conv_second(): taken = taken * same_seg[:, None, None]  23.8 us
  transfers between devices with their start and end apart: 11, of which 4 were waited for; matrix products, arithmetic and copies ran while one was open for 86% of the time, Pallas kernels for 0%

commit v1 on v0

--- a/solution.py
+++ b/solution.py
@@ -158,7 +158,10 @@
     bounds = jnp.cumsum(lengths[0])
     local_mel = mel_frames[0]
     first_base = index * frames_dev
-    second_full = lax.all_gather(w_second, ("rec", "tm"), axis=0, tiled=True)
+    second_full = jnp.concatenate(
+        lax.all_to_all(jnp.stack([w_second] * lax.axis_size(("rec", "tm"))), ("rec", "tm"), 0, 0),
+        axis=0,
+    )
     block_count = tokens_dev // CONV_BLOCK
     mel_edge = passed_along(local_mel[frames_dev - 3 :], "tm", 1)
     extended = jnp.concatenate([mel_edge, local_mel], axis=0)

time: 886 us -> 840 us (0.948)
  waiting for transfers between devices: 74 us -> 38.3 us
  local copies, waits for them, and re-layouts: 458 us -> 444 us
  starting transfers between devices: 14 us -> 25.8 us
    all_gather x1 -> x0, waiting for transfers between devices: 56.1 us -> none  [on_device(): second_full = lax.all_gather(w_second, ('rec', 'tm'), axis=0, tiled=True)]
    all_to_all x0 -> x1, waiting for transfers between devices: none -> 20.4 us  [on_device(): lax.all_to_all(jnp.stack([w_second] * lax.axis_size(('rec', 'tm'))), ('re...]
    all_to_all x0 -> x1, starting transfers between devices: none -> 10.2 us  [on_device(): lax.all_to_all(jnp.stack([w_second] * lax.axis_size(('rec', 'tm'))), ('re...]
  transfers between devices with their start and end apart: 11 -> 11, of which waited for: 4 -> 4; matrix products, arithmetic and copies ran while one was open for 86% -> 88% of each run, Pallas kernels for 0% -> 0%
where the time goes in v1:
time: 840 us; the launch traced here: 835 us
  local copies, waits for them, and re-layouts  444 us (53%)
  matrix products  201 us (24%)
  other arithmetic  99.5 us (12%)
  waiting for transfers between devices  38.3 us (5%)
  starting transfers between devices  25.8 us (3%)
  between operations  13.5 us (2%)
  loops' own time  12.7 us (2%)
    slice x72, local copies, waits for them, and re-layouts, conv_second(): taken[:, step_f:step_f + 2 * quarter - 1:2]  284 us
    dot_general x72, matrix products, conv_second(): jnp.dot(columns, w_second[offset:offset + channels], preferred_element_ty...  144 us
    convert_element_type x8, other arithmetic, conv_first(): return jnp.maximum(total, 0.0).astype(jnp.bfloat16)  61.5 us
    slice x72, local copies, waits for them, and re-layouts, conv_first(): columns = taken[:, step_f:step_f + bins - 1:2]  57.2 us
    reshape x72, local copies, waits for them, and re-layouts, conv_second(): taken[:, step_f:step_f + 2 * quarter - 1:2]  55.9 us
    dot_general x5, matrix products, add_product(): return jnp.dot(inputs, piece, preferred_element_type=jnp.float32)  31.1 us
    mul x8, other arithmetic, conv_second(): taken = taken * same_seg[:, None, None]  23.9 us
    all_to_all x1, waiting for transfers between devices, on_device(): lax.all_to_all(jnp.stack([w_second] * lax.axis_size(('rec', 'tm'))), ('re...  20.4 us
  transfers between devices with their start and end apart: 11, of which 4 were waited for; matrix products, arithmetic and copies ran while one was open for 88% of the time, Pallas kernels for 0%

profile of v1, /device:TPU:25, one launch (start us, length us, event | category | flops | bytes accessed | tf_op | source)
XLA Modules:
  0.0 834.7 jit_solution(8870315891327239908)
XLA Ops:
  15.9 10.2 %all-to-all-start = ((bf16[128,18,256]{2,1,0:T(8,128)(2,1)}), bf16[128,18,256]{2,1,0:T(8,128)(2,1)S(1)}, u32[]{:S(2)}, u32[]{:S(2)}) async-start(bf16[128,18,256]{2,1,0:T(8,128)(2,1)} %stack.2), calls=%async_computation | async-start | bytes 3145728 | tf_op jit(solution)/shard_map/all_to_all | solution.py:162
  28.4 20.4 %all-to-all-done = bf16[128,18,256]{2,1,0:T(8,128)(2,1)S(1)} async-done(((bf16[128,18,256]{2,1,0:T(8,128)(2,1)}), bf16[128,18,256]{2,1,0:T(8,128)(2,1)S(1)}, u32[]{:S(2)}, u32[]{:S(2)}) %all-to-all-start) | async-done | bytes 1179680 | tf_op jit(solution)/shard_map/all_to_all | solution.py:162
  50.0 667.4 %while.25 = (s32[]{:T(128)}, bf16[8,64,5120]{2,1,0:T(8,128)(2,1)}, s32[8]{0:T(128)S(1)}, bf16[2051,80]{1,0:T(8,128)(2,1)S(1)}, s32[]{:T(128)}, /*index=5*/s32[4]...) while((s32[]{:T(128)}, bf16[8,64,5120]{2,1,0:T(8,128)(2,1)}, ...), condition=%wide.region_3.4_spmd, body=%wide.region_1.3_spmd.sunk | while | flops 1543876352 | bytes 95192408 | solution.py:177
  59.7 7.7 maximum_convert_fusion.2
  71.1 6.9 slice.735
  84.1 4.9 slice.737
  92.7 4.8 slice.738
  104.4 4.9 slice.740
  112.9 4.7 slice.741
  124.6 4.9 slice.743
  143.4 7.7 maximum_convert_fusion.2
  154.8 6.9 slice.735
  167.6 4.9 slice.737
  176.2 4.8 slice.738
  187.8 4.9 slice.740
  196.4 4.7 slice.741
  208.0 4.9 slice.743
  226.8 7.7 maximum_convert_fusion.2
  238.2 6.9 slice.735
  251.0 4.9 slice.737
  259.6 4.8 slice.738
  271.3 4.9 slice.740
  279.8 4.7 slice.741
  291.6 4.9 slice.743
  310.3 7.7 maximum_convert_fusion.2
  321.7 6.9 slice.735
  334.5 4.9 slice.737
  343.0 4.8 slice.738
  354.7 4.9 slice.740
  363.3 4.7 slice.741
  374.9 4.9 slice.743
  393.7 7.7 maximum_convert_fusion.2
  405.1 6.9 slice.735
  417.8 4.9 slice.737
  426.4 4.8 slice.738
  438.1 4.9 slice.740
  446.7 4.7 slice.741
  458.3 4.9 slice.743
  477.0 7.7 maximum_convert_fusion.2
  488.4 6.9 slice.735
  501.2 4.9 slice.737
  509.8 4.8 slice.738
  521.5 4.9 slice.740
  530.0 4.7 slice.741
  541.7 4.9 slice.743
  560.4 7.7 maximum_convert_fusion.2
  571.8 6.9 slice.735
  584.5 4.9 slice.737
  593.1 4.8 slice.738
  604.8 4.9 slice.740
  613.4 4.7 slice.741
  625.0 4.9 slice.743
  643.7 7.7 maximum_convert_fusion.2
  655.1 6.9 slice.735
  667.9 4.9 slice.737
  676.5 4.8 slice.738
  688.2 4.9 slice.740
  708.4 4.9 slice.743
  717.5 10.0 %fusion.62 = (f32[512]{0:T(512)S(1)}, f32[512,1024]{1,0:T(8,128)S(1)}) fusion(bf16[512,5120]{1,0:T(8,128)(2,1)} %bitcast.117, bf16[5120,1024]{1,0:T(8,128)(2,1)} %all-gather.6.cloned.1.call-done), kind=kOutput, calls=%fused_computation.140 | convolution fusion | flops 5369232896 | bytes 17827840 | tf_op jit(solution)/shard_map/dot_general | solution.py:135
  728.2 6.6 convolution_convert_fusion.1
  734.9 5.6 collective-permute-start.1
  746.7 6.5 collective-permute-done.2
  755.0 46.4 %while.26 = (s32[]{:T(128)}, bf16[8,512,128]{1,2,0:T(8,128)(2,1)}, s32[8]{0:T(128)S(1)}, bf16[512,1024]{1,0:T(8,128)(2,1)S(1)}, bf16[768,2048]{1,0:T(8,128)(2,1)...) while((s32[]{:T(128)}, bf16[8,512,128]{1,2,0:T(8,128)(2,1)}, ...), condition=%wide.region_11.12_spmd.clone, body=%wide.region_8.11_spmd.clone.sunk | while | flops 212401152 | bytes 5925630 | solution.py:116
  820.2 6.0 fusion.64
  (737 shorter events, 438.1 us)
Async XLA Ops:
  6.5 710.9 %all-gather.6.cloned.1.call-start = ((), (), s32[]{:S(2)}) async-start(), calls=%async_computation.1 | async-start | bytes 10567680 | tf_op jit(solution)/shard_map/all_gather | solution.py:179
  7.3 720.6 %all-gather.8.cloned.1.call-start = ((), (), s32[]{:S(2)}) async-start(), calls=%async_computation.2 | async-start | bytes 6340608 | tf_op jit(solution)/shard_map/all_gather | solution.py:185
  8.0 793.4 %all-gather.10.cloned.1.call-start = ((), (), s32[]{:S(2)}) async-start(), calls=%async_computation.3 | async-start | bytes 2113536 | tf_op jit(solution)/shard_map/all_gather | solution.py:194
  8.7 796.9 %all-gather.12.cloned.1.call-start = ((), (), s32[]{:S(2)}) async-start(), calls=%async_computation.4 | async-start | bytes 4227072 | tf_op jit(solution)/shard_map/all_gather | solution.py:197
  10.6 16.1 %copy-start.20 = (s32[1,4]{1,0:T(1,128)S(1)}, s32[1,4]{1,0:T(1,128)}, u32[]{:S(2)}) copy-start(s32[1,4]{1,0:T(1,128)} %param.18) | copy-start | bytes 52
  10.6 17.6 %collective-permute-start = (bf16[3,80]{1,0:T(4,128)(2,1)S(1)}, bf16[3,80]{1,0:T(4,128)(2,1)S(1)}, u32[]{:S(2)}, u32[]{:S(2)}) collective-permute-start(bf16[3,80]{1,0:T(4,128)(2,1)S(1)} %slice_bitcast_fusion), channel_id=1, source_target_pairs={{0,1},{1,2},{2,3},{3,4},{4,5},{5,6},{6,7},{7,8},{8,9},{9,10},{10,1... | collective-permute-start | bytes 1448 | tf_op jit(solution)/shard_map/ppermute | solution.py:18
  15.9 32.9 %all-to-all-start = ((bf16[128,18,256]{2,1,0:T(8,128)(2,1)}), bf16[128,18,256]{2,1,0:T(8,128)(2,1)S(1)}, u32[]{:S(2)}, u32[]{:S(2)}) async-start(bf16[128,18,256]{2,1,0:T(8,128)(2,1)} %stack.2), calls=%async_computation | async-start | bytes 3145728 | tf_op jit(solution)/shard_map/all_to_all | solution.py:162
  26.0 24.0 %copy-start.9 = (f32[3,3,256]{2,1,0:T(4,128)S(1)}, f32[3,3,256]{2,1,0:T(4,128)}, u32[]{:S(2)}) copy-start(f32[3,3,256]{2,1,0:T(4,128)} %param.19) | copy-start | bytes 27652
  26.1 789.8 %all-gather.14.cloned.1.call-start = ((), (), s32[]{:S(2)}) async-start(), calls=%async_computation.5 | async-start | bytes 2113536 | tf_op jit(solution)/shard_map/all_gather | solution.py:204
  50.0 9.7 %copy-start.7 = (bf16[2051,80]{1,0:T(8,128)(2,1)}, bf16[2051,80]{1,0:T(8,128)(2,1)S(1)}, u32[]{:S(2)}) copy-start(bf16[2051,80]{1,0:T(8,128)(2,1)S(1)} %get-tuple-element.446) | copy-start | bytes 984484 | tf_op jit(solution)/shard_map/while
  50.0 9.7 %copy-start.12 = (s32[4]{0:T(128)}, s32[4]{0:T(128)S(1)}, u32[]{:S(2)}) copy-start(s32[4]{0:T(128)S(1)} %get-tuple-element.448) | copy-start | bytes 52 | tf_op jit(solution)/shard_map/while
  92.7 6.0 copy-start.4
  109.3 3.7 copy-start
  112.9 6.0 copy-start.3
  133.7 9.7 %copy-start.7 = (bf16[2051,80]{1,0:T(8,128)(2,1)}, bf16[2051,80]{1,0:T(8,128)(2,1)S(1)}, u32[]{:S(2)}) copy-start(bf16[2051,80]{1,0:T(8,128)(2,1)S(1)} %get-tuple-element.446) | copy-start | bytes 984484 | tf_op jit(solution)/shard_map/while
  133.7 9.7 %copy-start.12 = (s32[4]{0:T(128)}, s32[4]{0:T(128)S(1)}, u32[]{:S(2)}) copy-start(s32[4]{0:T(128)S(1)} %get-tuple-element.448) | copy-start | bytes 52 | tf_op jit(solution)/shard_map/while
  172.5 3.7 copy-start.1
  176.1 6.0 copy-start.4
  192.7 3.7 copy-start
  196.4 6.0 copy-start.3
  217.1 9.7 %copy-start.7 = (bf16[2051,80]{1,0:T(8,128)(2,1)}, bf16[2051,80]{1,0:T(8,128)(2,1)S(1)}, u32[]{:S(2)}) copy-start(bf16[2051,80]{1,0:T(8,128)(2,1)S(1)} %get-tuple-element.446) | copy-start | bytes 984484 | tf_op jit(solution)/shard_map/while
  217.2 9.7 %copy-start.12 = (s32[4]{0:T(128)}, s32[4]{0:T(128)S(1)}, u32[]{:S(2)}) copy-start(s32[4]{0:T(128)S(1)} %get-tuple-element.448) | copy-start | bytes 52 | tf_op jit(solution)/shard_map/while
  255.9 3.7 copy-start.1
  259.6 6.0 copy-start.4
  276.2 3.7 copy-start
  279.8 6.1 copy-start.3
  300.6 9.7 %copy-start.7 = (bf16[2051,80]{1,0:T(8,128)(2,1)}, bf16[2051,80]{1,0:T(8,128)(2,1)S(1)}, u32[]{:S(2)}) copy-start(bf16[2051,80]{1,0:T(8,128)(2,1)S(1)} %get-tuple-element.446) | copy-start | bytes 984484 | tf_op jit(solution)/shard_map/while
  300.6 9.7 %copy-start.12 = (s32[4]{0:T(128)}, s32[4]{0:T(128)S(1)}, u32[]{:S(2)}) copy-start(s32[4]{0:T(128)S(1)} %get-tuple-element.448) | copy-start | bytes 52 | tf_op jit(solution)/shard_map/while
  339.4 3.7 copy-start.1
  343.0 6.0 copy-start.4
  359.6 3.7 copy-start
  363.3 6.0 copy-start.3
  384.0 9.7 %copy-start.7 = (bf16[2051,80]{1,0:T(8,128)(2,1)}, bf16[2051,80]{1,0:T(8,128)(2,1)S(1)}, u32[]{:S(2)}) copy-start(bf16[2051,80]{1,0:T(8,128)(2,1)S(1)} %get-tuple-element.446) | copy-start | bytes 984484 | tf_op jit(solution)/shard_map/while
  384.0 9.7 %copy-start.12 = (s32[4]{0:T(128)}, s32[4]{0:T(128)S(1)}, u32[]{:S(2)}) copy-start(s32[4]{0:T(128)S(1)} %get-tuple-element.448) | copy-start | bytes 52 | tf_op jit(solution)/shard_map/while
  422.7 3.7 copy-start.1
  426.4 6.0 copy-start.4
  443.0 3.7 copy-start
  446.6 6.0 copy-start.3
  467.3 9.7 %copy-start.7 = (bf16[2051,80]{1,0:T(8,128)(2,1)}, bf16[2051,80]{1,0:T(8,128)(2,1)S(1)}, u32[]{:S(2)}) copy-start(bf16[2051,80]{1,0:T(8,128)(2,1)S(1)} %get-tuple-element.446) | copy-start | bytes 984484 | tf_op jit(solution)/shard_map/while
  467.3 9.7 %copy-start.12 = (s32[4]{0:T(128)}, s32[4]{0:T(128)S(1)}, u32[]{:S(2)}) copy-start(s32[4]{0:T(128)S(1)} %get-tuple-element.448) | copy-start | bytes 52 | tf_op jit(solution)/shard_map/while
  509.8 6.0 copy-start.4
  526.3 3.7 copy-start
  530.0 6.0 copy-start.3
  550.7 9.7 %copy-start.7 = (bf16[2051,80]{1,0:T(8,128)(2,1)}, bf16[2051,80]{1,0:T(8,128)(2,1)S(1)}, u32[]{:S(2)}) copy-start(bf16[2051,80]{1,0:T(8,128)(2,1)S(1)} %get-tuple-element.446) | copy-start | bytes 984484 | tf_op jit(solution)/shard_map/while
  550.7 9.7 %copy-start.12 = (s32[4]{0:T(128)}, s32[4]{0:T(128)S(1)}, u32[]{:S(2)}) copy-start(s32[4]{0:T(128)S(1)} %get-tuple-element.448) | copy-start | bytes 52 | tf_op jit(solution)/shard_map/while
  589.4 3.7 copy-start.1
  593.1 6.0 copy-start.4
  613.3 6.0 copy-start.3
  634.0 9.7 %copy-start.7 = (bf16[2051,80]{1,0:T(8,128)(2,1)}, bf16[2051,80]{1,0:T(8,128)(2,1)S(1)}, u32[]{:S(2)}) copy-start(bf16[2051,80]{1,0:T(8,128)(2,1)S(1)} %get-tuple-element.446) | copy-start | bytes 984484 | tf_op jit(solution)/shard_map/while
  634.1 9.7 %copy-start.12 = (s32[4]{0:T(128)}, s32[4]{0:T(128)S(1)}, u32[]{:S(2)}) copy-start(s32[4]{0:T(128)S(1)} %get-tuple-element.448) | copy-start | bytes 52 | tf_op jit(solution)/shard_map/while
  676.5 6.0 copy-start.4
  693.0 3.7 copy-start
  696.7 6.0 copy-start.3
  727.5 7.3 copy-start.6
  734.8 8.1 copy-start.5
  734.8 7.7 copy-start.14
  734.8 7.7 copy-start.16
  734.8 7.8 copy-start.10
  734.8 7.8 copy-start.11
  734.9 11.7 %collective-permute-start.1 = (bf16[128,2048]{1,0:T(8,128)(2,1)S(1)}, bf16[128,2048]{1,0:T(8,128)(2,1)S(1)}, u32[]{:S(2)}, u32[]{:S(2)}) collective-permute-start(bf16[128,2048]{1,0:T(8,128)(2,1)S(1)} %get-tuple-element.258), channel_id=1, source_target_pairs={{0,1},{1,2},{2,3},{3,4},{4,5},{5,6},{6,7},{7,8},{8,9},{9,10},{10,1... | collective-permute-start | bytes 1572872 | tf_op jit(solution)/shard_map/ppermute | solution.py:26
  740.6 12.6 %collective-permute-start.2 = (bf16[128,2048]{1,0:T(8,128)(2,1)S(1)}, bf16[128,2048]{1,0:T(8,128)(2,1)S(1)}, u32[]{:S(2)}, u32[]{:S(2)}) collective-permute-start(bf16[128,2048]{1,0:T(8,128)(2,1)S(1)} %get-tuple-element.259), channel_id=1, source_target_pairs={{1,0},{2,1},{3,2},{4,3},{5,4},{6,5},{7,6},{8,7},{9,8},{10,9},{11,1... | collective-permute-start | bytes 1572872 | tf_op jit(solution)/shard_map/ppermute | solution.py:29
  742.9 12.1 %slice-start = ((bf16[512,3072]{1,0:T(8,128)(2,1)}), bf16[512,1024]{1,0:T(8,128)(2,1)S(1)}, s32[]{:S(2)}) async-start(bf16[512,3072]{1,0:T(8,128)(2,1)} %copy-done.5), calls=%async_computation.6 | async-start | bytes 2097152 | tf_op jit(solution)/shard_map/slice | solution.py:188
  811.2 4.7 collective-permute-start.3
  813.1 7.1 collective-permute-start.4
  (48 other events, 89.1 us)
Sparse Core Ops, SparseCore 0:
  10.5 83.6 all-gather.5
  97.3 65.5 all-gather.7
  166.0 62.7 all-gather.9
  231.8 64.3 all-gather.11
  299.1 62.7 all-gather.13
